TPU v7x, 32 devices: a whole 2x2x4 slice. The times are simulated.
32 devices in a mesh: table: 8 (over z, y), helper: 4 (over x, core).
Axes of the slice: x: 2, y: 2, z: 4, core: 2. Of those that a mesh axis runs over, the one named last changes fastest.
Arguments:
- tables: bfloat16 [64, 4096, 128], P('table'), may hold values from -6 to 6
- projections: bfloat16 [64, 128, 256], P('table'), may hold values from -0.0234375 to 0.0234375
- bag_rows: int32 [64, 8, 4, 8, 16], P('table', None, 'helper'), may hold values from 0 to 4095
- bag_lengths: int32 [64, 8, 4, 8], P('table', None, 'helper'), may hold values from 1 to 16
- candidates: bfloat16 [8, 4, 2048, 256], P('table', 'helper'), may hold values from -6 to 6
- request_counts: int32 [8, 4, 8], P('table', 'helper'), may hold values from 1 to 1024, as said below
- cross_down: bfloat16 [3, 512, 128], replicated, may hold values from -0.25 to 0.25
- cross_up: bfloat16 [3, 128, 512], replicated, may hold values from -0.5 to 0.5
- cross_bias: float32 [3, 512], replicated, may hold values from -3 to 3
- layer_one: bfloat16 [512, 1024], replicated, may hold values from -0.25 to 0.25
- bias_one: float32 [1024], replicated, may hold values from -2 to 2
- layer_two: bfloat16 [1024, 512], replicated, may hold values from -0.1875 to 0.1875
- bias_two: float32 [512], replicated, may hold values from -2 to 2
- layer_three: bfloat16 [512, 256], replicated, may hold values from -0.25 to 0.25
- bias_three: float32 [256], replicated, may hold values from -2 to 2
- score_weight: bfloat16 [256], replicated, may hold values from -0.375 to 0.375
Outputs:
- scores: float32 [8, 4, 2048], P('table', 'helper')
Inputs may be any that keep to these rules, and one draw needn't show every extreme that they name: For each (a, h) the 8 counts request_counts[a, h, :] sum to at most 2048; for every a exactly one h has a sum of exactly 2048, and in that list the first request holds exactly 1024 candidates.
All inputs are finite; a program needn't handle non-finite values.
Results may differ from a plain program's by a relative error of at most 0.018.
Values may be sent and summed in bfloat16 or wider, within the bound.
A program may use at most 128 MiB of HBM per device.

v0:
```python
import jax
import jax.numpy as jnp
from jax import lax
from jax.sharding import PartitionSpec as P

BLOCK = 256


def cross_network(features, context_rows, live_slots, weights):
    (
        cross_down,
        cross_up,
        cross_bias,
        layer_one,
        bias_one,
        layer_two,
        bias_two,
        layer_three,
        bias_three,
        score_weight,
    ) = weights
    cross_input = jnp.concatenate([features, context_rows], axis=1)
    anchor = cross_input.astype(jnp.float32)
    current = anchor
    for layer_number in range(cross_down.shape[0]):
        reduced = jnp.dot(
            current.astype(jnp.bfloat16),
            cross_down[layer_number],
            preferred_element_type=jnp.float32,
        ).astype(jnp.bfloat16)
        current = (
            anchor
            * (
                jnp.dot(reduced, cross_up[layer_number], preferred_element_type=jnp.float32)
                + cross_bias[layer_number]
            )
            + current
        )
    hidden = jax.nn.relu(
        jnp.dot(current.astype(jnp.bfloat16), layer_one, preferred_element_type=jnp.float32)
        + bias_one
    ).astype(jnp.bfloat16)
    hidden = jax.nn.relu(
        jnp.dot(hidden, layer_two, preferred_element_type=jnp.float32) + bias_two
    ).astype(jnp.bfloat16)
    hidden = jax.nn.relu(
        jnp.dot(hidden, layer_three, preferred_element_type=jnp.float32) + bias_three
    ).astype(jnp.bfloat16)
    result = jnp.dot(hidden, score_weight, preferred_element_type=jnp.float32)
    return jnp.where(live_slots, result, jnp.zeros_like(result))


def context_lookup(codes, context):
    labels = jnp.arange(context.shape[0], dtype=jnp.int32)
    choose = (codes[:, None] == labels[None, :]).astype(jnp.bfloat16)
    return jnp.dot(choose, context, preferred_element_type=jnp.float32).astype(jnp.bfloat16)


def block_scores(features, codes, context, weights):
    return cross_network(features, context_lookup(codes, context), codes >= 0, weights)


def slot_codes(counts, total_slots):
    ends = jnp.cumsum(counts)
    positions = jnp.arange(total_slots, dtype=jnp.int32)
    owner = jnp.sum((positions[:, None] >= ends[None, :]).astype(jnp.int32), axis=1)
    return jnp.where(owner < counts.shape[0], owner, -1)


def pool_table(table, indices, lengths):
    table_rows = table.shape[0]
    flat_rows = indices.reshape(-1, indices.shape[-1])
    flat_lengths = lengths.reshape(-1)
    labels = jnp.arange(table_rows, dtype=jnp.int32)
    tally = jnp.zeros((flat_rows.shape[0], table_rows), jnp.float32)
    for position in range(flat_rows.shape[1]):
        chosen = jnp.where(flat_lengths > position, flat_rows[:, position], -1)
        tally = tally + (chosen[:, None] == labels[None, :]).astype(jnp.float32)
    return jnp.dot(tally.astype(jnp.bfloat16), table, preferred_element_type=jnp.float32).astype(
        jnp.bfloat16
    )


def body(
    tables,
    projections,
    bag_rows,
    bag_lengths,
    candidates,
    request_counts,
    cross_down,
    cross_up,
    cross_bias,
    layer_one,
    bias_one,
    layer_two,
    bias_two,
    layer_three,
    bias_three,
    score_weight,
):
    weights = (
        cross_down,
        cross_up,
        cross_bias,
        layer_one,
        bias_one,
        layer_two,
        bias_two,
        layer_three,
        bias_three,
        score_weight,
    )
    local_tables = tables.shape[0]
    owners = bag_rows.shape[1]
    requests = bag_rows.shape[3]
    width = projections.shape[2]
    pooled_list = []
    for table_number in range(local_tables):
        pooled_list.append(
            pool_table(tables[table_number], bag_rows[table_number], bag_lengths[table_number])
        )
    projected = jnp.stack(
        [
            jnp.dot(
                pooled_list[table_number],
                projections[table_number],
                preferred_element_type=jnp.float32,
            ).astype(jnp.bfloat16)
            for table_number in range(local_tables)
        ],
        axis=0,
    )
    projected = projected.reshape(local_tables, owners, requests, width)
    received = lax.all_to_all(projected, "table", split_axis=1, concat_axis=0, tiled=True)
    context = jnp.sum(received.astype(jnp.float32), axis=(0, 1)).astype(jnp.bfloat16)
    features = candidates[0, 0]
    total_slots = features.shape[0]
    blocks = total_slots // BLOCK
    codes = slot_codes(request_counts[0, 0], total_slots)

    def empty_block():
        return jnp.zeros((BLOCK,), jnp.float32)

    def own_block(pieces):
        block_features, block_codes = pieces
        return lax.cond(
            block_codes[0] >= 0,
            lambda: block_scores(block_features, block_codes, context, weights),
            empty_block,
        )

    scores = lax.map(
        own_block, (features.reshape(blocks, BLOCK, width), codes.reshape(blocks, BLOCK))
    )
    result = scores.reshape(total_slots)
    return result.reshape(1, 1, total_slots)


def solution(mesh):
    in_specs = (
        P("table", None, None),
        P("table", None, None),
        P("table", None, "helper", None, None),
        P("table", None, "helper", None),
        P("table", "helper", None, None),
        P("table", "helper", None),
        P(),
        P(),
        P(),
        P(),
        P(),
        P(),
        P(),
        P(),
        P(),
        P(),
    )
    out_specs = P("table", "helper", None)
    return jax.shard_map(body, mesh=mesh, in_specs=in_specs, out_specs=out_specs, check_vma=False)
```

profile of v0, /device:TPU:0, one launch (start us, length us, event | category | flops | bytes accessed | tf_op | source)
XLA Modules:
  0.0 134.6 jit_solution(14103113073700829227)
XLA Ops:
  0.0 2.2 %compare_reduce_fusion.10 = (pred[8,8]{1,0:T(8,128)(4,1)S(1)}, pred[8,8]{1,0:T(8,128)(4,1)S(1)}, pred[8,8]{1,0:T(8,128)(4,1)S(1)}, pred[8,8]{1,0:T(8,128)(4,1)S(...) fusion(s32[8,8,1,8]{3,2,1,0:T(1,128)} %param.23), kind=kLoop, calls=%fused_computation.401 | loop fusion | flops 5760 | bytes 7808 | tf_op jit(solution)/shard_map/gt | solution.py:77
  2.2 1.3 compare_reduce_fusion.11
  3.6 0.9 slice_bitcast_fusion
  28.9 4.2 %fusion.46 = bf16[8,8,8,256]{3,2,0,1:T(8,128)(2,1)} fusion(bf16[8,4096,128]{2,1,0:T(8,128)(2,1)} %param.20, s32[64]{0:T(128)S(1)} %get-tuple-element.593, s32[64]{0:T(128)S(1)} %get-tuple-element.594, s32[64]{0:T(128)S(1)} %get-tuple-element.595, s32[64]{0:T(128)S(1)} %get-tuple-element.596, s32[64]{0:T(128)S(1)} %get-tuple-element.597, ...), kind=kOutput, calls=%fused_computation.61 | convolution fusion | flops 83910656 | bytes 1155072 | tf_op jit(solution)/shard_map/dot_general | solution.py:125
  33.2 4.4 %fusion.48 = bf16[8,8,8,256]{3,2,0,1:T(8,128)(2,1)} fusion(bf16[8,8,8,256]{3,2,0,1:T(8,128)(2,1)} %fusion.46, bf16[8,4096,128]{2,1,0:T(8,128)(2,1)} %param.20, s32[64]{0:T(128)S(1)} %get-tuple-element.609, s32[64]{0:T(128)S(1)} %get-tuple-element.610, s32[64]{0:T(128)S(1)} %get-tuple-element.611, s32[64]{0:T(128)S(1)} %get-tuple-element.612, ...), kind=kOutput, calls=%fused_computation.63 | convolution fusion | flops 83910656 | bytes 1155072 | tf_op jit(solution)/shard_map/dot_general | solution.py:125
  37.5 4.2 %fusion.50 = bf16[8,8,8,256]{3,2,0,1:T(8,128)(2,1)} fusion(bf16[8,8,8,256]{3,2,0,1:T(8,128)(2,1)} %fusion.48, bf16[8,4096,128]{2,1,0:T(8,128)(2,1)} %param.20, s32[64]{0:T(128)S(1)} %get-tuple-element.625, s32[64]{0:T(128)S(1)} %get-tuple-element.626, s32[64]{0:T(128)S(1)} %get-tuple-element.627, s32[64]{0:T(128)S(1)} %get-tuple-element.628, ...), kind=kOutput, calls=%fused_computation.65 | convolution fusion | flops 83910656 | bytes 1155072 | tf_op jit(solution)/shard_map/dot_general | solution.py:125
  41.8 4.2 %fusion.52 = bf16[8,8,8,256]{3,2,0,1:T(8,128)(2,1)} fusion(bf16[8,8,8,256]{3,2,0,1:T(8,128)(2,1)} %fusion.50, bf16[8,4096,128]{2,1,0:T(8,128)(2,1)} %param.20, s32[64]{0:T(128)S(1)} %get-tuple-element.641, s32[64]{0:T(128)S(1)} %get-tuple-element.642, s32[64]{0:T(128)S(1)} %get-tuple-element.643, s32[64]{0:T(128)S(1)} %get-tuple-element.644, ...), kind=kOutput, calls=%fused_computation.67 | convolution fusion | flops 83910656 | bytes 1155072 | tf_op jit(solution)/shard_map/dot_general | solution.py:125
  46.0 4.2 %fusion.54 = bf16[8,8,8,256]{3,2,0,1:T(8,128)(2,1)} fusion(bf16[8,8,8,256]{3,2,0,1:T(8,128)(2,1)} %fusion.52, bf16[8,4096,128]{2,1,0:T(8,128)(2,1)} %param.20, s32[64]{0:T(128)S(1)} %get-tuple-element.657, s32[64]{0:T(128)S(1)} %get-tuple-element.658, s32[64]{0:T(128)S(1)} %get-tuple-element.659, s32[64]{0:T(128)S(1)} %get-tuple-element.660, ...), kind=kOutput, calls=%fused_computation.69 | convolution fusion | flops 83910656 | bytes 1155072 | tf_op jit(solution)/shard_map/dot_general | solution.py:125
  50.2 4.2 %fusion.56 = bf16[8,8,8,256]{3,2,0,1:T(8,128)(2,1)} fusion(bf16[8,8,8,256]{3,2,0,1:T(8,128)(2,1)} %fusion.54, bf16[8,4096,128]{2,1,0:T(8,128)(2,1)} %param.20, s32[64]{0:T(128)S(1)} %get-tuple-element.673, s32[64]{0:T(128)S(1)} %get-tuple-element.674, s32[64]{0:T(128)S(1)} %get-tuple-element.675, s32[64]{0:T(128)S(1)} %get-tuple-element.676, ...), kind=kOutput, calls=%fused_computation.71 | convolution fusion | flops 83910656 | bytes 1155072 | tf_op jit(solution)/shard_map/dot_general | solution.py:125
  54.4 4.3 %fusion.58 = bf16[8,8,8,256]{3,2,0,1:T(8,128)(2,1)} fusion(bf16[8,8,8,256]{3,2,0,1:T(8,128)(2,1)} %fusion.56, bf16[8,4096,128]{2,1,0:T(8,128)(2,1)} %param.20, s32[64]{0:T(128)S(1)} %get-tuple-element.689, s32[64]{0:T(128)S(1)} %get-tuple-element.690, s32[64]{0:T(128)S(1)} %get-tuple-element.691, s32[64]{0:T(128)S(1)} %get-tuple-element.692, ...), kind=kOutput, calls=%fused_computation.73 | convolution fusion | flops 83910656 | bytes 1155072 | tf_op jit(solution)/shard_map/dot_general | solution.py:125
  58.7 4.5 %fusion.60 = bf16[8,8,8,256]{3,2,0,1:T(8,128)(2,1)} fusion(bf16[8,8,8,256]{3,2,0,1:T(8,128)(2,1)} %fusion.58, bf16[8,4096,128]{2,1,0:T(8,128)(2,1)} %param.20, s32[64]{0:T(128)S(1)} %get-tuple-element.705, s32[64]{0:T(128)S(1)} %get-tuple-element.706, s32[64]{0:T(128)S(1)} %get-tuple-element.707, s32[64]{0:T(128)S(1)} %get-tuple-element.708, ...), kind=kOutput, calls=%fused_computation.75 | convolution fusion | flops 83910656 | bytes 1155072 | tf_op jit(solution)/shard_map/dot_general | solution.py:125
  63.2 7.3 %all-to-all-start = ((bf16[8,8,8,256]{3,2,0,1:T(8,128)(2,1)}), bf16[8,8,8,256]{3,2,0,1:T(8,128)(2,1)S(1)}, u32[]{:S(2)}, u32[]{:S(2)}) async-start(bf16[8,8,8,256]{3,2,0,1:T(8,128)(2,1)} %fusion.60), calls=%async_computation | async-start | bytes 524288 | tf_op jit(solution)/shard_map/all_to_all | solution.py:135
  70.5 0.5 copy.437
  71.4 8.1 %all-to-all-done = bf16[8,8,8,256]{3,2,0,1:T(8,128)(2,1)S(1)} async-done(((bf16[8,8,8,256]{3,2,0,1:T(8,128)(2,1)}), bf16[8,8,8,256]{3,2,0,1:T(8,128)(2,1)S(1)}, u32[]{:S(2)}, u32[]{:S(2)}) %all-to-all-start) | async-done | bytes 262176 | tf_op jit(solution)/shard_map/all_to_all | solution.py:135
  79.6 54.4 %while.10 = (s32[]{:T(128)}, f32[8,256]{1,0:T(8,128)S(1)}, s32[8,256]{1,0:T(8,128)S(1)}, bf16[8,256,256]{1,2,0:T(8,128)(2,1)S(1)}, bf16[8,256]{1,0:T(8,128)(2,1)...) while((s32[]{:T(128)}, f32[8,256]{1,0:T(8,128)S(1)}, ...), condition=%wide.region_6.7_spmd, body=%wide.region_3.6_spmd.sunk | while | flops 811698688 | bytes 8822575 | solution.py:153
  79.6 0.6 fusion.383
  80.9 5.4 %conditional.2 = (f32[1,256]{1,0:T(1,128)S(1)}) conditional(s32[]{:T(128)} %bitcast.417, () %tuple.437, (s32[1,256]{1,0:T(1,128)S(1)}, bf16[8,256,256]{1,2,0:T(8,128)(2,1)S(1)}, s32[]{:T(128)}, bf16[8,256]{1,0:T(8,128)(2,1)S(1)}, bf16[3,512,128]{2,1,0:T(8,128)(2,1)S(1)}, /*index=5*/bf16[3,128,512]{2,1,0:T(8,128)(2,1)S(1)}, f32[3,512]{1,0:T(4,128)S(1)}, ...), branch_computations={%region_4.4_spmd, %region_5.5_spmd} | conditional | flops 811698688 | bytes 8818188 | solution.py:147
  81.7 0.5 fusion.6
  82.2 0.5 fusion.9
  82.7 2.3 %fusion.10 = bf16[256,512]{1,0:T(8,128)(2,1)S(1)} fusion(bf16[1024,512]{1,0:T(8,128)(2,1)} %get-tuple-element.138, bf16[256,512]{0,1:T(8,128)(2,1)S(1)} %fusion.9, bf16[512,1024]{1,0:T(8,128)(2,1)} %get-tuple-element.136, f32[1024]{0:T(1024)S(1)} %get-tuple-element.137, f32[512]{0:T(512)S(1)} %get-tuple-element.139), kind=kOutput, calls=%fused_computation.15 | convolution fusion | flops 538050560 | bytes 2627584 | tf_op jit(solution)/shard_map/while/body/eval_jaxpr/cond/branch_1_fun/dot_general | solution.py:44
  85.0 1.3 fusion.13
  86.4 0.6 fusion.383
  87.7 5.4 %conditional.2 = (f32[1,256]{1,0:T(1,128)S(1)}) conditional(s32[]{:T(128)} %bitcast.417, () %tuple.437, (s32[1,256]{1,0:T(1,128)S(1)}, bf16[8,256,256]{1,2,0:T(8,128)(2,1)S(1)}, s32[]{:T(128)}, bf16[8,256]{1,0:T(8,128)(2,1)S(1)}, bf16[3,512,128]{2,1,0:T(8,128)(2,1)S(1)}, /*index=5*/bf16[3,128,512]{2,1,0:T(8,128)(2,1)S(1)}, f32[3,512]{1,0:T(4,128)S(1)}, ...), branch_computations={%region_4.4_spmd, %region_5.5_spmd} | conditional | flops 811698688 | bytes 8818188 | solution.py:147
  88.0 0.5 fusion.4
  88.5 0.5 fusion.6
  89.5 2.3 %fusion.10 = bf16[256,512]{1,0:T(8,128)(2,1)S(1)} fusion(bf16[1024,512]{1,0:T(8,128)(2,1)} %get-tuple-element.138, bf16[256,512]{0,1:T(8,128)(2,1)S(1)} %fusion.9, bf16[512,1024]{1,0:T(8,128)(2,1)} %get-tuple-element.136, f32[1024]{0:T(1024)S(1)} %get-tuple-element.137, f32[512]{0:T(512)S(1)} %get-tuple-element.139), kind=kOutput, calls=%fused_computation.15 | convolution fusion | flops 538050560 | bytes 2627584 | tf_op jit(solution)/shard_map/while/body/eval_jaxpr/cond/branch_1_fun/dot_general | solution.py:44
  91.8 1.3 fusion.13
  93.2 0.6 fusion.383
  94.5 5.4 %conditional.2 = (f32[1,256]{1,0:T(1,128)S(1)}) conditional(s32[]{:T(128)} %bitcast.417, () %tuple.437, (s32[1,256]{1,0:T(1,128)S(1)}, bf16[8,256,256]{1,2,0:T(8,128)(2,1)S(1)}, s32[]{:T(128)}, bf16[8,256]{1,0:T(8,128)(2,1)S(1)}, bf16[3,512,128]{2,1,0:T(8,128)(2,1)S(1)}, /*index=5*/bf16[3,128,512]{2,1,0:T(8,128)(2,1)S(1)}, f32[3,512]{1,0:T(4,128)S(1)}, ...), branch_computations={%region_4.4_spmd, %region_5.5_spmd} | conditional | flops 811698688 | bytes 8818188 | solution.py:147
  94.8 0.5 fusion.4
  95.3 0.5 fusion.6
  96.3 2.3 %fusion.10 = bf16[256,512]{1,0:T(8,128)(2,1)S(1)} fusion(bf16[1024,512]{1,0:T(8,128)(2,1)} %get-tuple-element.138, bf16[256,512]{0,1:T(8,128)(2,1)S(1)} %fusion.9, bf16[512,1024]{1,0:T(8,128)(2,1)} %get-tuple-element.136, f32[1024]{0:T(1024)S(1)} %get-tuple-element.137, f32[512]{0:T(512)S(1)} %get-tuple-element.139), kind=kOutput, calls=%fused_computation.15 | convolution fusion | flops 538050560 | bytes 2627584 | tf_op jit(solution)/shard_map/while/body/eval_jaxpr/cond/branch_1_fun/dot_general | solution.py:44
  98.6 1.3 fusion.13
  100.0 0.6 fusion.383
  101.3 5.4 %conditional.2 = (f32[1,256]{1,0:T(1,128)S(1)}) conditional(s32[]{:T(128)} %bitcast.417, () %tuple.437, (s32[1,256]{1,0:T(1,128)S(1)}, bf16[8,256,256]{1,2,0:T(8,128)(2,1)S(1)}, s32[]{:T(128)}, bf16[8,256]{1,0:T(8,128)(2,1)S(1)}, bf16[3,512,128]{2,1,0:T(8,128)(2,1)S(1)}, /*index=5*/bf16[3,128,512]{2,1,0:T(8,128)(2,1)S(1)}, f32[3,512]{1,0:T(4,128)S(1)}, ...), branch_computations={%region_4.4_spmd, %region_5.5_spmd} | conditional | flops 811698688 | bytes 8818188 | solution.py:147
  101.6 0.5 fusion.4
  102.1 0.5 fusion.6
  103.1 2.3 %fusion.10 = bf16[256,512]{1,0:T(8,128)(2,1)S(1)} fusion(bf16[1024,512]{1,0:T(8,128)(2,1)} %get-tuple-element.138, bf16[256,512]{0,1:T(8,128)(2,1)S(1)} %fusion.9, bf16[512,1024]{1,0:T(8,128)(2,1)} %get-tuple-element.136, f32[1024]{0:T(1024)S(1)} %get-tuple-element.137, f32[512]{0:T(512)S(1)} %get-tuple-element.139), kind=kOutput, calls=%fused_computation.15 | convolution fusion | flops 538050560 | bytes 2627584 | tf_op jit(solution)/shard_map/while/body/eval_jaxpr/cond/branch_1_fun/dot_general | solution.py:44
  105.4 1.3 fusion.13
  106.8 0.6 fusion.383
  108.1 5.4 %conditional.2 = (f32[1,256]{1,0:T(1,128)S(1)}) conditional(s32[]{:T(128)} %bitcast.417, () %tuple.437, (s32[1,256]{1,0:T(1,128)S(1)}, bf16[8,256,256]{1,2,0:T(8,128)(2,1)S(1)}, s32[]{:T(128)}, bf16[8,256]{1,0:T(8,128)(2,1)S(1)}, bf16[3,512,128]{2,1,0:T(8,128)(2,1)S(1)}, /*index=5*/bf16[3,128,512]{2,1,0:T(8,128)(2,1)S(1)}, f32[3,512]{1,0:T(4,128)S(1)}, ...), branch_computations={%region_4.4_spmd, %region_5.5_spmd} | conditional | flops 811698688 | bytes 8818188 | solution.py:147
  108.4 0.5 fusion.4
  108.9 0.5 fusion.6
  109.9 2.3 %fusion.10 = bf16[256,512]{1,0:T(8,128)(2,1)S(1)} fusion(bf16[1024,512]{1,0:T(8,128)(2,1)} %get-tuple-element.138, bf16[256,512]{0,1:T(8,128)(2,1)S(1)} %fusion.9, bf16[512,1024]{1,0:T(8,128)(2,1)} %get-tuple-element.136, f32[1024]{0:T(1024)S(1)} %get-tuple-element.137, f32[512]{0:T(512)S(1)} %get-tuple-element.139), kind=kOutput, calls=%fused_computation.15 | convolution fusion | flops 538050560 | bytes 2627584 | tf_op jit(solution)/shard_map/while/body/eval_jaxpr/cond/branch_1_fun/dot_general | solution.py:44
  112.2 1.3 fusion.13
  113.6 0.6 fusion.383
  114.9 5.4 %conditional.2 = (f32[1,256]{1,0:T(1,128)S(1)}) conditional(s32[]{:T(128)} %bitcast.417, () %tuple.437, (s32[1,256]{1,0:T(1,128)S(1)}, bf16[8,256,256]{1,2,0:T(8,128)(2,1)S(1)}, s32[]{:T(128)}, bf16[8,256]{1,0:T(8,128)(2,1)S(1)}, bf16[3,512,128]{2,1,0:T(8,128)(2,1)S(1)}, /*index=5*/bf16[3,128,512]{2,1,0:T(8,128)(2,1)S(1)}, f32[3,512]{1,0:T(4,128)S(1)}, ...), branch_computations={%region_4.4_spmd, %region_5.5_spmd} | conditional | flops 811698688 | bytes 8818188 | solution.py:147
  115.2 0.5 fusion.4
  115.7 0.5 fusion.6
  116.7 2.3 %fusion.10 = bf16[256,512]{1,0:T(8,128)(2,1)S(1)} fusion(bf16[1024,512]{1,0:T(8,128)(2,1)} %get-tuple-element.138, bf16[256,512]{0,1:T(8,128)(2,1)S(1)} %fusion.9, bf16[512,1024]{1,0:T(8,128)(2,1)} %get-tuple-element.136, f32[1024]{0:T(1024)S(1)} %get-tuple-element.137, f32[512]{0:T(512)S(1)} %get-tuple-element.139), kind=kOutput, calls=%fused_computation.15 | convolution fusion | flops 538050560 | bytes 2627584 | tf_op jit(solution)/shard_map/while/body/eval_jaxpr/cond/branch_1_fun/dot_general | solution.py:44
  119.0 1.3 fusion.13
  120.4 0.6 fusion.383
  121.7 5.4 %conditional.2 = (f32[1,256]{1,0:T(1,128)S(1)}) conditional(s32[]{:T(128)} %bitcast.417, () %tuple.437, (s32[1,256]{1,0:T(1,128)S(1)}, bf16[8,256,256]{1,2,0:T(8,128)(2,1)S(1)}, s32[]{:T(128)}, bf16[8,256]{1,0:T(8,128)(2,1)S(1)}, bf16[3,512,128]{2,1,0:T(8,128)(2,1)S(1)}, /*index=5*/bf16[3,128,512]{2,1,0:T(8,128)(2,1)S(1)}, f32[3,512]{1,0:T(4,128)S(1)}, ...), branch_computations={%region_4.4_spmd, %region_5.5_spmd} | conditional | flops 811698688 | bytes 8818188 | solution.py:147
  122.0 0.5 fusion.4
  122.5 0.5 fusion.6
  123.5 2.3 %fusion.10 = bf16[256,512]{1,0:T(8,128)(2,1)S(1)} fusion(bf16[1024,512]{1,0:T(8,128)(2,1)} %get-tuple-element.138, bf16[256,512]{0,1:T(8,128)(2,1)S(1)} %fusion.9, bf16[512,1024]{1,0:T(8,128)(2,1)} %get-tuple-element.136, f32[1024]{0:T(1024)S(1)} %get-tuple-element.137, f32[512]{0:T(512)S(1)} %get-tuple-element.139), kind=kOutput, calls=%fused_computation.15 | convolution fusion | flops 538050560 | bytes 2627584 | tf_op jit(solution)/shard_map/while/body/eval_jaxpr/cond/branch_1_fun/dot_general | solution.py:44
  125.8 1.3 fusion.13
  127.2 0.6 fusion.383
  128.5 5.4 %conditional.2 = (f32[1,256]{1,0:T(1,128)S(1)}) conditional(s32[]{:T(128)} %bitcast.417, () %tuple.437, (s32[1,256]{1,0:T(1,128)S(1)}, bf16[8,256,256]{1,2,0:T(8,128)(2,1)S(1)}, s32[]{:T(128)}, bf16[8,256]{1,0:T(8,128)(2,1)S(1)}, bf16[3,512,128]{2,1,0:T(8,128)(2,1)S(1)}, /*index=5*/bf16[3,128,512]{2,1,0:T(8,128)(2,1)S(1)}, f32[3,512]{1,0:T(4,128)S(1)}, ...), branch_computations={%region_4.4_spmd, %region_5.5_spmd} | conditional | flops 811698688 | bytes 8818188 | solution.py:147
  128.8 0.5 fusion.4
  129.3 0.5 fusion.6
  130.3 2.3 %fusion.10 = bf16[256,512]{1,0:T(8,128)(2,1)S(1)} fusion(bf16[1024,512]{1,0:T(8,128)(2,1)} %get-tuple-element.138, bf16[256,512]{0,1:T(8,128)(2,1)S(1)} %fusion.9, bf16[512,1024]{1,0:T(8,128)(2,1)} %get-tuple-element.136, f32[1024]{0:T(1024)S(1)} %get-tuple-element.137, f32[512]{0:T(512)S(1)} %get-tuple-element.139), kind=kOutput, calls=%fused_computation.15 | convolution fusion | flops 538050560 | bytes 2627584 | tf_op jit(solution)/shard_map/while/body/eval_jaxpr/cond/branch_1_fun/dot_general | solution.py:44
  132.6 1.3 fusion.13
  133.9 0.6 reshape_reshape.3
  (418 shorter events, 30.8 us)
Async XLA Ops:
  0.0 28.9 %copy-start.4 = (bf16[8,128,256]{2,1,0:T(8,128)(2,1)S(1)}, bf16[8,128,256]{2,1,0:T(8,128)(2,1)}, u32[]{:S(2)}) copy-start(bf16[8,128,256]{2,1,0:T(8,128)(2,1)} %param.21) | copy-start | bytes 1572868
  54.4 16.1 %copy-start.2 = (bf16[1,1,2048,256]{3,2,1,0:T(8,128)(2,1)S(1)}, bf16[1,1,2048,256]{3,2,1,0:T(8,128)(2,1)}, u32[]{:S(2)}) copy-start(bf16[1,1,2048,256]{3,2,1,0:T(8,128)(2,1)} %param.24) | copy-start | bytes 3145732
  54.4 16.7 %copy-start.8 = (s32[1,1,8]{2,1,0:T(1,128)S(1)}, s32[1,1,8]{2,1,0:T(1,128)}, u32[]{:S(2)}) copy-start(s32[1,1,8]{2,1,0:T(1,128)} %param.25) | copy-start | bytes 100
  58.7 20.8 %copy-start = (bf16[3,512,128]{2,1,0:T(8,128)(2,1)S(1)}, bf16[3,512,128]{2,1,0:T(8,128)(2,1)}, u32[]{:S(2)}) copy-start(bf16[3,512,128]{2,1,0:T(8,128)(2,1)} %param.26) | copy-start | bytes 1179652
  58.7 20.8 %copy-start.1 = (bf16[3,128,512]{2,1,0:T(8,128)(2,1)S(1)}, bf16[3,128,512]{2,1,0:T(8,128)(2,1)}, u32[]{:S(2)}) copy-start(bf16[3,128,512]{2,1,0:T(8,128)(2,1)} %param.27) | copy-start | bytes 1179652
  58.7 20.8 %copy-start.3 = (f32[3,512]{1,0:T(4,128)S(1)}, f32[3,512]{1,0:T(4,128)}, u32[]{:S(2)}) copy-start(f32[3,512]{1,0:T(4,128)} %param.28) | copy-start | bytes 18436
  58.7 20.8 %copy-start.5 = (f32[1024]{0:T(1024)S(1)}, f32[1024]{0:T(1024)}, u32[]{:S(2)}) copy-start(f32[1024]{0:T(1024)} %param.30) | copy-start | bytes 12292
  58.7 20.9 %copy-start.6 = (f32[512]{0:T(512)S(1)}, f32[512]{0:T(512)}, u32[]{:S(2)}) copy-start(f32[512]{0:T(512)} %param.32) | copy-start | bytes 6148
  58.7 20.9 %copy-start.7 = (f32[256]{0:T(256)S(1)}, f32[256]{0:T(256)}, u32[]{:S(2)}) copy-start(f32[256]{0:T(256)} %param.34) | copy-start | bytes 3076
  58.7 20.9 %copy-start.9 = (bf16[256]{0:T(256)(128)(2,1)S(1)}, bf16[256]{0:T(256)(128)(2,1)}, u32[]{:S(2)}) copy-start(bf16[256]{0:T(256)(128)(2,1)} %param.35) | copy-start | bytes 1540
  63.2 16.2 %all-to-all-start = ((bf16[8,8,8,256]{3,2,0,1:T(8,128)(2,1)}), bf16[8,8,8,256]{3,2,0,1:T(8,128)(2,1)S(1)}, u32[]{:S(2)}, u32[]{:S(2)}) async-start(bf16[8,8,8,256]{3,2,0,1:T(8,128)(2,1)} %fusion.60), calls=%async_computation | async-start | bytes 524288 | tf_op jit(solution)/shard_map/all_to_all | solution.py:135
where the time goes:
time: 135 us
  matrix products  76.8 us (57%)
  local copies, waits for them, and re-layouts  26 us (19%)
  other arithmetic  9.15 us (7%)
  waiting for transfers between devices  8.07 us (6%)
  starting transfers between devices  7.31 us (5%)
  loops' own time  6.45 us (5%)
    dot_general x8, matrix products, body(): jnp.dot(pooled_list[table_number], projections[table_number], preferred_e...  34.2 us
    dot_general x8, matrix products, cross_network(): jnp.dot(hidden, layer_two, preferred_element_type=jnp.float32) + bias_two  18.3 us
    gt x128, local copies, waits for them, and re-layouts, pool_table(): chosen = jnp.where(flat_lengths > position, flat_rows[:, position], -1)  12.5 us
    dot_general x24, matrix products, cross_network(): jnp.dot(reduced, cross_up[layer_number], preferred_element_type=jnp.float32)  11.7 us
    dot_general x8, matrix products, cross_network(): result = jnp.dot(hidden, score_weight, preferred_element_type=jnp.float32)  10.4 us
    unnamed x148, local copies, waits for them, and re-layouts  9.31 us
    all_to_all x1, waiting for transfers between devices, body(): lax.all_to_all(projected, 'table', split_axis=1, concat_axis=0, tiled=True)  8.07 us
    all_to_all x1, starting transfers between devices, body(): lax.all_to_all(projected, 'table', split_axis=1, concat_axis=0, tiled=True)  7.31 us
  transfers between devices with their start and end apart: 1, of which 1 were waited for; matrix products, arithmetic and copies ran while one was open for 1% of the time, Pallas kernels for 0%

commit v1 on v0

v1 whole, which is shorter than its diff:
```python
import functools

import jax
import jax.numpy as jnp
from jax import lax
from jax.experimental import pallas as pl
from jax.experimental.pallas import tpu as pltpu
from jax.sharding import PartitionSpec as P

GROUP = 16
SUB = 256
CHAINS = 2


def lane_dot(left, right):
    return lax.dot_general(
        left, right, (((1,), (1,)), ((), ())), preferred_element_type=jnp.float32
    )


def dot(left, right):
    return jnp.dot(left, right, preferred_element_type=jnp.float32)


def kernel(
    peers,
    bag,
    counts_ref,
    hi_ref,
    lo_ref,
    tables_hbm,
    proj_hbm,
    cand_hbm,
    down_hbm,
    up_hbm,
    one_hbm,
    two_hbm,
    three_hbm,
    cross_bias_ref,
    bias_one_ref,
    bias_two_ref,
    bias_three_ref,
    score_ref,
    out_ref,
    tables_v,
    proj_v,
    cand_v,
    down_v,
    up_v,
    one_v,
    two_v,
    three_v,
    tally,
    send,
    recv,
    context_v,
    table_sem,
    load_sem,
    send_sem,
    recv_sem,
):
    me = lax.axis_index("table")
    local_tables, rows, width = tables_v.shape
    requests = send.shape[1]
    bags = peers * requests
    groups = bags // GROUP
    lo_size = 256
    hi_size = rows // lo_size
    slots = cand_v.shape[0]

    loads = [
        pltpu.make_async_copy(source, target, load_sem.at[number])
        for number, (source, target) in enumerate(
            (
                (proj_hbm, proj_v),
                (cand_hbm, cand_v),
                (down_hbm, down_v),
                (up_hbm, up_v),
                (one_hbm, one_v),
                (two_hbm, two_v),
                (three_hbm, three_v),
            )
        )
    ]

    def table_copy(number):
        return pltpu.make_async_copy(
            tables_hbm.at[number], tables_v.at[number], table_sem.at[number]
        )

    for number in range(local_tables):
        table_copy(number).start()
    for load in loads:
        load.start()

    barrier = pltpu.get_barrier_semaphore()

    def greet(step, carry):
        peer = lax.rem(me + step, peers)
        pl.semaphore_signal(barrier, inc=1, device_id={"table": peer})
        return carry

    lax.fori_loop(1, peers, greet, 0)

    hi_labels = lax.broadcasted_iota(jnp.int32, (hi_size * GROUP, GROUP * bag), 0).astype(
        jnp.float32
    ).astype(jnp.bfloat16)
    lo_labels = lax.broadcasted_iota(jnp.int32, (lo_size, GROUP * bag), 0).astype(
        jnp.float32
    ).astype(jnp.bfloat16)
    one = jnp.ones((), jnp.bfloat16)
    zero = jnp.zeros((), jnp.bfloat16)

    loads[0].wait()
    total = jnp.zeros((bags, proj_v.shape[2]), jnp.float32)
    for number in range(local_tables):
        for group in range(groups):
            hi = hi_ref[number, pl.ds(group, 1), :]
            lo = lo_ref[number, pl.ds(group, 1), :]
            left = jnp.where(hi_labels == hi, one, zero)
            right = jnp.where(lo_labels == lo, one, zero)
            part = lane_dot(left, right).astype(jnp.bfloat16)
            for high in range(hi_size):
                tally[
                    number % 2,
                    pl.ds(group * GROUP, GROUP),
                    pl.ds(high * lo_size, lo_size),
                ] = part[high * GROUP : (high + 1) * GROUP]
        table_copy(number).wait()
        pooled = dot(tally[number % 2], tables_v[number]).astype(jnp.bfloat16)
        total = total + dot(pooled, proj_v[number])
    send[...] = total.reshape(send.shape)

    pl.semaphore_wait(barrier, peers - 1)

    def remote(step):
        peer = lax.rem(me + step, peers)
        return pltpu.make_async_remote_copy(
            src_ref=send.at[peer],
            dst_ref=recv.at[step],
            send_sem=send_sem.at[step],
            recv_sem=recv_sem.at[step],
            device_id={"table": peer},
        )

    def start(step, carry):
        remote(step).start()
        return carry

    def finish(step, summed):
        remote(step).wait()
        return summed + recv[step]

    lax.fori_loop(1, peers, start, 0)
    for load in loads[1:]:
        load.wait()
    summed = lax.fori_loop(1, peers, finish, send[me])
    context_v[...] = summed.astype(jnp.bfloat16)

    lanes = lax.broadcasted_iota(jnp.int32, (1, requests), 1)
    starts = jnp.zeros((1, requests), jnp.int32)
    ends = jnp.zeros((1, requests), jnp.int32)
    live_total = 0
    for request in range(requests):
        count = counts_ref[0, 0, request]
        starts = starts + jnp.where(lanes > request, count, 0)
        ends = ends + jnp.where(lanes >= request, count, 0)
        live_total = live_total + count

    def tower(first):
        slot = first + lax.broadcasted_iota(jnp.int32, (SUB, requests), 0)
        choose = jnp.where((slot >= starts) & (slot < ends), 1.0, 0.0).astype(jnp.bfloat16)
        context_rows = dot(choose, context_v[...])
        features = cand_v[pl.ds(first, SUB), :].astype(jnp.float32)
        anchor = jnp.concatenate([features, context_rows], axis=1)
        current = anchor
        for layer in range(down_v.shape[0]):
            reduced = dot(current.astype(jnp.bfloat16), down_v[layer]).astype(jnp.bfloat16)
            current = (
                anchor * (dot(reduced, up_v[layer]) + cross_bias_ref[layer : layer + 1, :])
                + current
            )
        hidden = jnp.maximum(
            dot(current.astype(jnp.bfloat16), one_v[...]) + bias_one_ref[...], 0.0
        ).astype(jnp.bfloat16)
        hidden = jnp.maximum(dot(hidden, two_v[...]) + bias_two_ref[...], 0.0).astype(
            jnp.bfloat16
        )
        hidden = jnp.maximum(dot(hidden, three_v[...]) + bias_three_ref[...], 0.0).astype(
            jnp.bfloat16
        )
        result = lane_dot(score_ref[...], hidden)
        position = first + lax.broadcasted_iota(jnp.int32, (1, SUB), 1)
        out_ref[:, pl.ds(first, SUB)] = jnp.where(position < live_total, result, 0.0)

    def step(number, carry):
        for chain in range(CHAINS):
            tower(pl.multiple_of((number * CHAINS + chain) * SUB, SUB))
        return carry

    lax.fori_loop(0, slots // (SUB * CHAINS), step, 0)


def body(
    peers,
    tables,
    projections,
    bag_rows,
    bag_lengths,
    candidates,
    request_counts,
    cross_down,
    cross_up,
    cross_bias,
    layer_one,
    bias_one,
    layer_two,
    bias_two,
    layer_three,
    bias_three,
    score_weight,
):
    local_tables, rows, width = tables.shape
    owners, requests, bag = bag_rows.shape[1], bag_rows.shape[3], bag_rows.shape[4]
    groups = owners * requests // GROUP
    features = candidates[0, 0]
    slots, pwidth = features.shape
    keep = jnp.arange(bag, dtype=jnp.int32) < bag_lengths[..., None]
    bag_number = jnp.arange(owners * requests, dtype=jnp.int32).reshape(owners, 1, requests, 1)
    hi = jnp.where(keep, (bag_rows // 256) * GROUP + bag_number % GROUP, -1)
    lo = bag_rows % 256
    hi = hi.astype(jnp.bfloat16).reshape(local_tables, groups, GROUP * bag)
    lo = lo.astype(jnp.bfloat16).reshape(local_tables, groups, GROUP * bag)
    vmem = pl.BlockSpec(memory_space=pltpu.VMEM)
    hbm = pl.BlockSpec(memory_space=pl.ANY)
    smem = pl.BlockSpec(memory_space=pltpu.SMEM)
    big = (tables, projections, features, cross_down, cross_up, layer_one, layer_two, layer_three)
    scores = pl.pallas_call(
        functools.partial(kernel, peers, bag),
        out_shape=jax.ShapeDtypeStruct((1, slots), jnp.float32),
        in_specs=[smem, vmem, vmem] + [hbm] * 8 + [vmem] * 5,
        out_specs=vmem,
        scratch_shapes=[pltpu.VMEM(array.shape, array.dtype) for array in big]
        + [
            pltpu.VMEM((2, owners * requests, rows), jnp.bfloat16),
            pltpu.VMEM((owners, requests, pwidth), jnp.float32),
            pltpu.VMEM((owners, requests, pwidth), jnp.float32),
            pltpu.VMEM((requests, pwidth), jnp.bfloat16),
            pltpu.SemaphoreType.DMA((local_tables,)),
            pltpu.SemaphoreType.DMA((7,)),
            pltpu.SemaphoreType.DMA((owners,)),
            pltpu.SemaphoreType.DMA((owners,)),
        ],
        compiler_params=pltpu.CompilerParams(
            collective_id=0, has_side_effects=True, vmem_limit_bytes=60 * 1024 * 1024
        ),
        name="rank_step",
    )(
        request_counts,
        hi,
        lo,
        *big,
        cross_bias,
        bias_one.reshape(1, -1),
        bias_two.reshape(1, -1),
        bias_three.reshape(1, -1),
        score_weight.reshape(1, -1),
    )
    return scores.reshape(1, 1, slots)


def solution(mesh):
    in_specs = (
        P("table", None, None),
        P("table", None, None),
        P("table", None, "helper", None, None),
        P("table", None, "helper", None),
        P("table", "helper", None, None),
        P("table", "helper", None),
    ) + (P(),) * 10
    out_specs = P("table", "helper", None)
    return jax.shard_map(
        functools.partial(body, mesh.shape["table"]),
        mesh=mesh,
        in_specs=in_specs,
        out_specs=out_specs,
        check_vma=False,
    )
```

time: 135 us -> 36.1 us (0.27)
  matrix products: 76.8 us -> 0 us
  Pallas kernels: 0 us -> 30.5 us
  local copies, waits for them, and re-layouts: 26 us -> 4.02 us
  waiting for transfers between devices: 8.07 us -> 0 us
  other arithmetic: 9.15 us -> 1.27 us
  starting transfers between devices: 7.31 us -> 0 us
  loops' own time: 6.45 us -> 0 us
    dot_general x56 -> x0, matrix products: 76.8 us -> none  [the longest x8 34.2 us: body(): jnp.dot(pooled_list[table_number], projections[table_number], preferred_e...]
    pallas_call x0 -> x1, Pallas kernels: none -> 30.5 us  [body(): pl.pallas_call(functools.partial(kernel, peers, bag), out_shape=jax.Shape...]
    gt x128 -> x0, local copies, waits for them, and re-layouts: 12.5 us -> none  [pool_table(): chosen = jnp.where(flat_lengths > position, flat_rows[:, position], -1)]
    all_to_all x1 -> x0, waiting for transfers between devices: 8.07 us -> none  [body(): lax.all_to_all(projected, 'table', split_axis=1, concat_axis=0, tiled=True)]
    unnamed x148 -> x1, local copies, waits for them, and re-layouts: 9.31 us -> 1.3 us
    all_to_all x1 -> x0, starting transfers between devices: 7.31 us -> none  [body(): lax.all_to_all(projected, 'table', split_axis=1, concat_axis=0, tiled=True)]
    another operation x9 -> x0, loops' own time: 6.45 us -> none  [the longest x1 5.8 us: body(): lax.map(own_block, (features.reshape(blocks, BLOCK, width), codes.reshape...]
    ge x8 -> x0, other arithmetic: 4.83 us -> none  [own_block(): block_codes[0] >= 0]
  transfers between devices with their start and end apart: 1 -> 0, of which waited for: 1 -> 0; matrix products, arithmetic and copies ran while one was open for 1% -> 0% of each run, Pallas kernels for 0% -> 0%
where the time goes in v1:
time: 36.1 us; the launch traced here: 35.8 us
  Pallas kernels  30.5 us (84%)
  local copies, waits for them, and re-layouts  4.02 us (11%)
  other arithmetic  1.27 us (4%)
    pallas_call x1, Pallas kernels, body(): pl.pallas_call(functools.partial(kernel, peers, bag), out_shape=jax.Shape...  30.5 us
    unnamed x1, local copies, waits for them, and re-layouts  1.3 us
    convert_element_type x1, other arithmetic, body(): lo = lo.astype(jnp.bfloat16).reshape(local_tables, groups, GROUP * bag)  1.26 us
    reshape x1, local copies, waits for them, and re-layouts, body(): score_weight.reshape(1, -1)  1.22 us
    reshape x1, local copies, waits for them, and re-layouts, body(): hi = hi.astype(jnp.bfloat16).reshape(local_tables, groups, GROUP * bag)  0.75 us
    reshape x1, local copies, waits for them, and re-layouts, body(): lo = lo.astype(jnp.bfloat16).reshape(local_tables, groups, GROUP * bag)  0.75 us

profile of v1, /device:TPU:0, one launch (start us, length us, event | category | flops | bytes accessed | tf_op | source)
XLA Modules:
  0.0 35.8 jit_solution(6664486404383069597)
XLA Ops:
  0.0 1.3 %fusion.4 = (bf16[8,8,1,8,16]{4,3,2,1,0:T(8,128)(2,1)S(1)}, bf16[8,8,1,8,16]{4,3,2,1,0:T(8,128)(2,1)S(1)}) fusion(s32[8,8,1,8,16]{4,3,2,1,0:T(8,128)} %param.18, s32[8,8]{1,0:T(8,128)S(1)} %add_select_fusion.2, s32[8,8,8]{2,1,0:T(8,128)} %bitcast.11), kind=kLoop, calls=%fused_computation.9 | loop fusion | flops 204800 | bytes 67840 | tf_op jit(solution)/shard_map/convert_element_type | solution.py:233
  1.3 0.8 %reshape.76.hi_ref = bf16[8,4,256]{2,1,0:T(4,128)(2,1)} reshape(bf16[8,8,1,8,16]{4,3,2,1,0:T(8,128)(2,1)S(1)} %get-tuple-element.6) | data formatting | bytes 32768 | tf_op jit(solution)/shard_map/reshape | solution.py:232
  2.0 0.8 %reshape.77.lo_ref = bf16[8,4,256]{2,1,0:T(4,128)(2,1)} reshape(bf16[8,8,1,8,16]{4,3,2,1,0:T(8,128)(2,1)S(1)} %get-tuple-element.5) | data formatting | bytes 32768 | tf_op jit(solution)/shard_map/reshape | solution.py:233
  2.8 1.2 %reshape.81.score_ref = bf16[1,256]{1,0:T(2,128)(2,1)} reshape(bf16[256]{0:T(256)(128)(2,1)} %param.31) | data formatting | bytes 1024 | tf_op jit(solution)/shard_map/reshape | solution.py:267
  4.0 30.5 %rank_step.1 = f32[1,2048]{1,0:T(1,128)} custom-call(s32[1,1,8]{2,1,0:T(1,128)} %counts_ref.1, bf16[8,4,256]{2,1,0:T(4,128)(2,1)} %reshape.76.hi_ref, bf16[8,4,256]{2,1,0:T(4,128)(2,1)} %reshape.77.lo_ref, bf16[8,4096,128]{2,1,0:T(8,128)(2,1)} %tables_hbm.1, bf16[8,128,256]{2,1,0:T(8,128)(2,1)} %proj_hbm.1, bf16[2048,256]{1,0:T(8,128)(2,1)} %bitcast.10, ...), custom_call_target="tpu_custom_call" | custom-call | tf_op jit(solution)/shard_map/rank_step/pallas_call | solution.py:238
  34.5 1.3 %copy.18 = f32[1,1,2048]{2,1,0:T(1,128)} copy(f32[1,1,2048]{2,1,0:T(1,128)} %bitcast.12) | data formatting | bytes 16384
  (1 shorter events, 0.0 us)

commit v2 on v1

--- a/solution.py
+++ b/solution.py
@@ -7,9 +7,10 @@
 from jax.experimental.pallas import tpu as pltpu
 from jax.sharding import PartitionSpec as P
 
-GROUP = 16
-SUB = 256
-CHAINS = 2
+DEPTH = 256
+TALLY_BYTES = 8 << 20
+SUB = 1024
+CHAINS = 1
 
 
 def lane_dot(left, right):
@@ -25,9 +26,9 @@
 def kernel(
     peers,
     bag,
-    counts_ref,
-    hi_ref,
-    lo_ref,
+    counts_hbm,
+    rows_hbm,
+    lengths_hbm,
     tables_hbm,
     proj_hbm,
     cand_hbm,
@@ -36,12 +37,15 @@
     one_hbm,
     two_hbm,
     three_hbm,
-    cross_bias_ref,
-    bias_one_ref,
-    bias_two_ref,
-    bias_three_ref,
-    score_ref,
+    cross_bias_hbm,
+    bias_one_hbm,
+    bias_two_hbm,
+    bias_three_hbm,
+    score_hbm,
     out_ref,
+    counts_ref,
+    rows_ref,
+    lengths_ref,
     tables_v,
     proj_v,
     cand_v,
@@ -50,6 +54,13 @@
     one_v,
     two_v,
     three_v,
+    cross_bias_ref,
+    bias_one_ref,
+    bias_two_ref,
+    bias_three_ref,
+    score_ref,
+    hi_v,
+    lo_v,
     tally,
     send,
     recv,
@@ -63,35 +74,77 @@
     local_tables, rows, width = tables_v.shape
     requests = send.shape[1]
     bags = peers * requests
-    groups = bags // GROUP
+    together = DEPTH // (requests * bag)
+    group_bags = together * requests
+    groups = peers // together
     lo_size = 256
     hi_size = rows // lo_size
     slots = cand_v.shape[0]
 
-    loads = [
-        pltpu.make_async_copy(source, target, load_sem.at[number])
-        for number, (source, target) in enumerate(
-            (
-                (proj_hbm, proj_v),
-                (cand_hbm, cand_v),
-                (down_hbm, down_v),
-                (up_hbm, up_v),
-                (one_hbm, one_v),
-                (two_hbm, two_v),
-                (three_hbm, three_v),
-            )
-        )
-    ]
+    def copies(pairs, offset):
+        return [
+            pltpu.make_async_copy(source, target, load_sem.at[offset + number])
+            for number, (source, target) in enumerate(pairs)
+        ]
+
+    first_loads = copies(((rows_hbm, rows_ref), (lengths_hbm, lengths_ref), (proj_hbm, proj_v)), 0)
+    late_loads = copies(
+        (
+            (counts_hbm, counts_ref),
+            (cand_hbm, cand_v),
+            (down_hbm, down_v),
+            (up_hbm, up_v),
+            (one_hbm, one_v),
+            (two_hbm, two_v),
+            (three_hbm, three_v),
+            (cross_bias_hbm, cross_bias_ref),
+            (bias_one_hbm, bias_one_ref),
+            (bias_two_hbm, bias_two_ref),
+            (bias_three_hbm, bias_three_ref),
+            (score_hbm, score_ref),
+        ),
+        3,
+    )
 
     def table_copy(number):
         return pltpu.make_async_copy(
             tables_hbm.at[number], tables_v.at[number], table_sem.at[number]
         )
 
+    for load in first_loads:
+        load.start()
     for number in range(local_tables):
         table_copy(number).start()
-    for load in loads:
-        load.start()
+
+    def code_rows():
+        span = requests * bag
+        raw = rows_ref[...]
+        pick = lax.broadcasted_iota(jnp.int32, (bag, span), 0)
+        lane = lax.broadcasted_iota(jnp.int32, (bag, span), 1)
+        spread = jnp.where(pick == lane % bag, 1.0, 0.0).astype(jnp.bfloat16)
+        pick = lax.broadcasted_iota(jnp.int32, (requests, span), 0)
+        lane = lax.broadcasted_iota(jnp.int32, (requests, span), 1)
+        own = pick == lane // bag
+        spread_lengths = jnp.where(own, 1.0, 0.0).astype(jnp.bfloat16)
+
+        def flat(values):
+            wide = dot(values.astype(jnp.float32).astype(jnp.bfloat16), spread)
+            wide = wide.reshape(values.shape[0] // requests, requests, span)
+            return jnp.sum(jnp.where(own[None], wide, 0.0), axis=1)
+
+        hi = flat(raw // lo_size)
+        lo = flat(raw % lo_size)
+        lengths = dot(lengths_ref[...].astype(jnp.float32).astype(jnp.bfloat16), spread_lengths)
+        lane = lax.broadcasted_iota(jnp.int32, hi.shape, 1)
+        line = lax.broadcasted_iota(jnp.int32, hi.shape, 0)
+        place = (line % together) * requests + lane // bag
+        keep = (lane % bag).astype(jnp.float32) < lengths
+        hi_v[...] = jnp.where(keep, hi * group_bags + place.astype(jnp.float32), -1.0)
+        lo_v[...] = lo
+
+    def joined(source, first):
+        pieces = [source[pl.ds(first + n, 1), :] for n in range(together)]
+        return jnp.concatenate(pieces, axis=1).astype(jnp.bfloat16)
 
     barrier = pltpu.get_barrier_semaphore()
 
@@ -102,33 +155,44 @@
 
     lax.fori_loop(1, peers, greet, 0)
 
-    hi_labels = lax.broadcasted_iota(jnp.int32, (hi_size * GROUP, GROUP * bag), 0).astype(
-        jnp.float32
-    ).astype(jnp.bfloat16)
-    lo_labels = lax.broadcasted_iota(jnp.int32, (lo_size, GROUP * bag), 0).astype(
-        jnp.float32
-    ).astype(jnp.bfloat16)
+    for load in first_loads:
+        load.wait()
+    code_rows()
+
+    def labels(count):
+        numbers = lax.broadcasted_iota(jnp.int32, (count, DEPTH), 0)
+        return numbers.astype(jnp.float32).astype(jnp.bfloat16)
+
+    hi_labels = labels(hi_size * group_bags)
+    lo_labels = labels(lo_size)
     one = jnp.ones((), jnp.bfloat16)
     zero = jnp.zeros((), jnp.bfloat16)
 
-    loads[0].wait()
-    total = jnp.zeros((bags, proj_v.shape[2]), jnp.float32)
-    for number in range(local_tables):
+    def fill(number):
         for group in range(groups):
-            hi = hi_ref[number, pl.ds(group, 1), :]
-            lo = lo_ref[number, pl.ds(group, 1), :]
+            first = number * peers + group * together
+            hi = joined(hi_v, first)
+            lo = joined(lo_v, first)
             left = jnp.where(hi_labels == hi, one, zero)
             right = jnp.where(lo_labels == lo, one, zero)
             part = lane_dot(left, right).astype(jnp.bfloat16)
             for high in range(hi_size):
                 tally[
-                    number % 2,
-                    pl.ds(group * GROUP, GROUP),
+                    number % tally.shape[0],
+                    pl.ds(group * group_bags, group_bags),
                     pl.ds(high * lo_size, lo_size),
-                ] = part[high * GROUP : (high + 1) * GROUP]
+                ] = part[high * group_bags : (high + 1) * group_bags]
+
+    ahead = tally.shape[0]
+    for number in range(ahead):
+        fill(number)
+    total = jnp.zeros((bags, proj_v.shape[2]), jnp.float32)
+    for number in range(local_tables):
         table_copy(number).wait()
-        pooled = dot(tally[number % 2], tables_v[number]).astype(jnp.bfloat16)
+        pooled = dot(tally[number % tally.shape[0]], tables_v[number]).astype(jnp.bfloat16)
         total = total + dot(pooled, proj_v[number])
+        if number + ahead < local_tables:
+            fill(number + ahead)
     send[...] = total.reshape(send.shape)
 
     pl.semaphore_wait(barrier, peers - 1)
@@ -152,7 +216,9 @@
         return summed + recv[step]
 
     lax.fori_loop(1, peers, start, 0)
-    for load in loads[1:]:
+    for load in late_loads:
+        load.start()
+    for load in late_loads:
         load.wait()
     summed = lax.fori_loop(1, peers, finish, send[me])
     context_v[...] = summed.astype(jnp.bfloat16)
@@ -189,7 +255,7 @@
         hidden = jnp.maximum(dot(hidden, three_v[...]) + bias_three_ref[...], 0.0).astype(
             jnp.bfloat16
         )
-        result = lane_dot(score_ref[...], hidden)
+        result = lane_dot(score_ref[...].reshape(1, -1), hidden)
         position = first + lax.broadcasted_iota(jnp.int32, (1, SUB), 1)
         out_ref[:, pl.ds(first, SUB)] = jnp.where(position < live_total, result, 0.0)
 
@@ -222,32 +288,46 @@
 ):
     local_tables, rows, width = tables.shape
     owners, requests, bag = bag_rows.shape[1], bag_rows.shape[3], bag_rows.shape[4]
-    groups = owners * requests // GROUP
     features = candidates[0, 0]
     slots, pwidth = features.shape
-    keep = jnp.arange(bag, dtype=jnp.int32) < bag_lengths[..., None]
-    bag_number = jnp.arange(owners * requests, dtype=jnp.int32).reshape(owners, 1, requests, 1)
-    hi = jnp.where(keep, (bag_rows // 256) * GROUP + bag_number % GROUP, -1)
-    lo = bag_rows % 256
-    hi = hi.astype(jnp.bfloat16).reshape(local_tables, groups, GROUP * bag)
-    lo = lo.astype(jnp.bfloat16).reshape(local_tables, groups, GROUP * bag)
     vmem = pl.BlockSpec(memory_space=pltpu.VMEM)
     hbm = pl.BlockSpec(memory_space=pl.ANY)
-    smem = pl.BlockSpec(memory_space=pltpu.SMEM)
-    big = (tables, projections, features, cross_down, cross_up, layer_one, layer_two, layer_three)
+    operands = (
+        request_counts,
+        bag_rows.reshape(-1, bag),
+        bag_lengths.reshape(-1, requests),
+        tables,
+        projections,
+        features,
+        cross_down,
+        cross_up,
+        layer_one,
+        layer_two,
+        layer_three,
+        cross_bias,
+        bias_one.reshape(1, -1),
+        bias_two.reshape(1, -1),
+        bias_three.reshape(1, -1),
+        score_weight,
+    )
+    room = TALLY_BYTES // (owners * requests * rows * 2)
+    ahead = min(local_tables, max(1, room))
     scores = pl.pallas_call(
         functools.partial(kernel, peers, bag),
         out_shape=jax.ShapeDtypeStruct((1, slots), jnp.float32),
-        in_specs=[smem, vmem, vmem] + [hbm] * 8 + [vmem] * 5,
+        in_specs=[hbm] * len(operands),
         out_specs=vmem,
-        scratch_shapes=[pltpu.VMEM(array.shape, array.dtype) for array in big]
+        scratch_shapes=[pltpu.SMEM(request_counts.shape, jnp.int32)]
+        + [pltpu.VMEM(array.shape, array.dtype) for array in operands[1:]]
         + [
-            pltpu.VMEM((2, owners * requests, rows), jnp.bfloat16),
+            pltpu.VMEM((local_tables * owners, requests * bag), jnp.float32),
+            pltpu.VMEM((local_tables * owners, requests * bag), jnp.float32),
+            pltpu.VMEM((ahead, owners * requests, rows), jnp.bfloat16),
             pltpu.VMEM((owners, requests, pwidth), jnp.float32),
             pltpu.VMEM((owners, requests, pwidth), jnp.float32),
             pltpu.VMEM((requests, pwidth), jnp.bfloat16),
             pltpu.SemaphoreType.DMA((local_tables,)),
-            pltpu.SemaphoreType.DMA((7,)),
+            pltpu.SemaphoreType.DMA((len(operands) - 1,)),
             pltpu.SemaphoreType.DMA((owners,)),
             pltpu.SemaphoreType.DMA((owners,)),
         ],
@@ -255,17 +335,7 @@
             collective_id=0, has_side_effects=True, vmem_limit_bytes=60 * 1024 * 1024
         ),
         name="rank_step",
-    )(
-        request_counts,
-        hi,
-        lo,
-        *big,
-        cross_bias,
-        bias_one.reshape(1, -1),
-        bias_two.reshape(1, -1),
-        bias_three.reshape(1, -1),
-        score_weight.reshape(1, -1),
-    )
+    )(*operands)
     return scores.reshape(1, 1, slots)
 
 

time: 36.1 us -> 26.9 us (0.75)
  Pallas kernels: 30.5 us -> 25.4 us
  local copies, waits for them, and re-layouts: 4.02 us -> 1.3 us
  other arithmetic: 1.27 us -> 0 us
    pallas_call x1, Pallas kernels: 30.5 us -> 25.4 us  [body(): pl.pallas_call(functools.partial(kernel, peers, bag), out_shape=jax.Shape...]
    reshape x3 -> x0, local copies, waits for them, and re-layouts: 2.72 us -> none  [the longest x1 1.22 us: body(): score_weight.reshape(1, -1)]
    convert_element_type x1 -> x0, other arithmetic: 1.26 us -> none  [body(): lo = lo.astype(jnp.bfloat16).reshape(local_tables, groups, GROUP * bag)]
where the time goes in v2:
time: 26.9 us; the launch traced here: 26.7 us
  Pallas kernels  25.4 us (94%)
  local copies, waits for them, and re-layouts  1.3 us (5%)
    pallas_call x1, Pallas kernels, body(): pl.pallas_call(functools.partial(kernel, peers, bag), out_shape=jax.Shape...  25.4 us
    unnamed x1, local copies, waits for them, and re-layouts  1.3 us

profile of v2, /device:TPU:0, one launch (start us, length us, event | category | flops | bytes accessed | tf_op | source)
XLA Modules:
  0.0 26.7 jit_solution(1167417510096576190)
XLA Ops:
  0.0 25.4 %rank_step.1 = f32[1,2048]{1,0:T(1,128)} custom-call(s32[1,1,8]{2,1,0:T(1,128)} %counts_hbm.1, s32[512,16]{1,0:T(8,128)} %bitcast.8, s32[64,8]{1,0:T(8,128)} %bitcast.9, bf16[8,4096,128]{2,1,0:T(8,128)(2,1)} %tables_hbm.1, bf16[8,128,256]{2,1,0:T(8,128)(2,1)} %proj_hbm.1, bf16[2048,256]{1,0:T(8,128)(2,1)} %bitcast.7, bf16[3,512,128]{2,1,0:T(8,128)(2,1)} %down_hbm.1, ...), custom_call_target="tpu_custom_call" | custom-call | tf_op jit(solution)/shard_map/rank_step/pallas_call | solution.py:315
  25.4 1.3 %copy.18 = f32[1,1,2048]{2,1,0:T(1,128)} copy(f32[1,1,2048]{2,1,0:T(1,128)} %bitcast.10) | data formatting | bytes 16384
